TPU v7x, 32 devices: a whole 2x2x4 slice. The times are simulated.
32 devices in a mesh: role: 2 (over y), tile: 16 (over z, x, core).
Axes of the slice: x: 2, y: 2, z: 4, core: 2. Of those that a mesh axis runs over, the one named last changes fastest.
Arguments:
- fields_pair: float32 [2, 512, 16384], P('role', None, 'tile'), may hold values from 0 to 1
- velocity: float32 [16384], P('tile'), may hold values from -0.5 to 0.5
- growth: float32 [16384], P('tile'), may hold values from 0.05 to 0.5
- features: bfloat16 [512, 1024], replicated, may hold values from -6 to 6
- assignment: int32 [512], replicated, may hold values from 0 to 511, each once
- out_pair: float32 [2, 1024, 16384], P('role', None, 'tile'), may hold values from -0.1875 to 0.1875
- hidden_pair: float32 [2, 5, 1024, 1024], P('role', None, 'tile'), may hold values from -0.1875 to 0.1875
Outputs:
- fields_next: float32 [2, 512, 16384], P('role', None, 'tile')
- out_next: float32 [2, 1024, 16384], P('role', None, 'tile')
- hidden_next: float32 [2, 5, 1024, 1024], P('role', None, 'tile')
Inputs may be any that keep to these rules, and one draw needn't show every extreme that they name: `assignment`: a permutation of the 512 members.
All inputs are finite; a program needn't handle non-finite values.
Results may differ from a plain program's by a relative error of at most 0.0022.
The roundings to bfloat16 on the way count: a program that leaves them out, or rounds other values in their place, can miss the bound.
Values may be sent and summed in bfloat16 or wider, within the bound.
A program may use at most 192 MiB of HBM per device.

v0:
```python
import jax
import jax.numpy as jnp
from jax import lax
from jax.sharding import PartitionSpec as P

BATCH = 512
momentum_decay = 0.9
step_size = 0.1


def extended(value, sides, width):
    for axis, dim in sides:
        count, length = (lax.axis_size(axis), value.shape[dim])
        up = [(i, (i + 1) % count) for i in range(count)]
        down = [(j, i) for i, j in up]
        last = lax.slice_in_dim(value, length - width, length, axis=dim)
        leading = lax.slice_in_dim(value, 0, width, axis=dim)
        before = lax.ppermute(last, axis, up)
        after = lax.ppermute(leading, axis, down)
        value = jnp.concatenate([before, value, after], axis=dim)
    return value


def spread(block, axis, owner):
    block = jnp.where(lax.axis_index(axis) == owner, block, jnp.zeros_like(block))
    return lax.psum(block, axis)


def partner(value, axis, distance):
    return lax.ppermute(value, axis, [(i, i ^ 1 << distance) for i in range(lax.axis_size(axis))])


def guarded(flag, action, *operands):

    def skipped(*values):
        return jax.tree.map(jnp.zeros_like, action(*values))

    return lax.cond(flag, action, skipped, *operands)


def silu_slope(values):
    logistic = jax.nn.sigmoid(values)
    return logistic * (1.0 + values * (1.0 - logistic))


def advance(padded, growth):
    states = padded[:-1]
    velocity_row = padded[-1]
    outflow = (
        jnp.maximum(velocity_row[:-1], 0.0) * states[:, :-1]
        + jnp.minimum(velocity_row[:-1], 0.0) * states[:, 1:]
    )
    carried = states[:, 1:-1] - outflow[:, 1:] + outflow[:, :-1]
    return carried + growth * carried * (1.0 - carried)


def body(fields_pair, velocity, growth, features, assignment, out_pair, hidden_pair):
    solver_side = lax.axis_index("role") == 0
    trainer_side = jnp.logical_not(solver_side)
    own_fields = fields_pair[0]
    own_out = out_pair[0]
    own_hidden = hidden_pair[0]
    layer_count = own_hidden.shape[0]
    unit_rows = own_hidden.shape[1]
    first_unit = lax.axis_index("tile") * unit_rows
    stacked = jnp.concatenate([own_fields, velocity[None, :]], axis=0)
    padded = extended(stacked, (("tile", 1),), 1)
    advanced = guarded(solver_side, advance, padded, growth)
    fresh_fields = spread(advanced, "role", 0)
    out_narrow = own_out.astype(jnp.bfloat16)
    hidden_narrow = own_hidden.astype(jnp.bfloat16)
    full_hidden = lax.all_gather(hidden_narrow, "tile", axis=1, tiled=True)

    def forward(features, full_hidden, out_narrow, target):
        inputs = []
        summed_list = []
        activation = features
        for layer_index in range(layer_count):
            inputs.append(activation)
            summed = jnp.dot(
                activation, full_hidden[layer_index], preferred_element_type=jnp.float32
            )
            summed_list.append(summed)
            activation = jax.nn.silu(summed).astype(jnp.bfloat16)
        predicted = jnp.dot(activation, out_narrow, preferred_element_type=jnp.float32)
        residual = ((predicted - target) / BATCH).astype(jnp.bfloat16)
        grad_out = jnp.dot(activation.T, residual, preferred_element_type=jnp.float32)
        partial_grad = lax.dot_general(
            residual, out_narrow, (((1,), (1,)), ((), ())), preferred_element_type=jnp.float32
        )
        return (jnp.stack(summed_list), jnp.stack(inputs), grad_out, partial_grad)

    summed_all, inputs_all, grad_out, partial_grad = guarded(
        trainer_side, forward, features, full_hidden, out_narrow, own_fields
    )
    upstream = lax.psum(partial_grad, "tile")

    def backward(summed_all, inputs_all, upstream, full_hidden, first_unit):
        gradients = []
        for layer_index in reversed(range(layer_count)):
            slope = (upstream * silu_slope(summed_all[layer_index])).astype(jnp.bfloat16)
            own_inputs = lax.dynamic_slice_in_dim(inputs_all[layer_index], first_unit, unit_rows, 1)
            gradients.append(jnp.dot(own_inputs.T, slope, preferred_element_type=jnp.float32))
            if layer_index > 0:
                upstream = lax.dot_general(
                    slope,
                    full_hidden[layer_index],
                    (((1,), (1,)), ((), ())),
                    preferred_element_type=jnp.float32,
                )
        return jnp.stack(gradients[::-1])

    grad_hidden = guarded(
        trainer_side, backward, summed_all, inputs_all, upstream, full_hidden, first_unit
    )
    solver_pack = jnp.concatenate([own_out.reshape(-1), own_hidden.reshape(-1)])
    trainer_pack = jnp.concatenate([grad_out.reshape(-1), grad_hidden.reshape(-1)])
    payload = jnp.where(solver_side, solver_pack, trainer_pack)
    received = partner(payload, "role", 0)
    out_length = own_out.size
    other_out = received[:out_length].reshape(own_out.shape)
    other_hidden = received[out_length:].reshape(own_hidden.shape)
    out_next = jnp.where(
        solver_side,
        momentum_decay * own_out + other_out,
        own_out - step_size * (momentum_decay * other_out + grad_out),
    )
    hidden_next = jnp.where(
        solver_side,
        momentum_decay * own_hidden + other_hidden,
        own_hidden - step_size * (momentum_decay * other_hidden + grad_hidden),
    )
    fields_next = jnp.where(solver_side, advanced, jnp.take(fresh_fields, assignment, axis=0))
    return (fields_next[None], out_next[None], hidden_next[None])


def solution(mesh):
    return jax.shard_map(
        body,
        mesh=mesh,
        in_specs=(
            P("role", None, "tile"),
            P("tile"),
            P("tile"),
            P(),
            P(),
            P("role", None, "tile"),
            P("role", None, "tile", None),
        ),
        out_specs=(P("role", None, "tile"), P("role", None, "tile"), P("role", None, "tile", None)),
        check_vma=False,
    )
```

profile of v0, /device:TPU:0, one launch (start us, length us, event | category | flops | bytes accessed | tf_op | source)
XLA Modules:
  0.0 473.0 jit_solution(12022284242264037515)
XLA Ops:
  8.1 2.4 bitcast_convert_fusion
  10.5 91.3 %all-gather.2.cloned.1.call-done = bf16[5,1024,1024]{2,1,0:T(8,128)(2,1)} async-done(((bf16[5,64,1024]{2,1,0:T(8,128)(2,1)}), bf16[5,1024,1024]{2,1,0:T(8,128)(2,1)}) %all-gather.2.cloned.1.call-update) | async-done | bytes 10485776 | tf_op jit(solution)/shard_map/all_gather | solution.py:72
  101.9 14.5 %conditional.4 = (f32[5,512,1024]{2,1,0:T(8,128)}, bf16[5,512,1024]{2,1,0:T(8,128)(2,1)}, f32[1024,1024]{1,0:T(8,128)}, f32[512,1024]{1,0:T(8,128)}, f32[1048576]{0:T(1024)}) conditional(s32[]{:T(128)} %convert_element_type.53, () %tuple.39, (bf16[5,1024,1024]{2,1,0:T(8,128)(2,1)}, bf16[512,1024]{1,0:T(8,128)(2,1)}, f32[1024,1024]{1,0:T(8,128)}, ...), branch_computations={%region_3.4_spmd, %region_4.5_spmd} | conditional | flops 8619819008 | bytes 140509344 | solution.py:38
  101.9 5.2 %broadcast.47 = f32[5,512,1024]{2,1,0:T(8,128)} broadcast(f32[]{:T(128)} %constant.41.clone), dimensions={} | broadcast | bytes 10485764 | tf_op jit(solution)/shard_map/broadcast.16
  107.1 3.0 broadcast.48
  110.1 2.5 broadcast.49
  112.6 2.2 reshape.52
  114.8 1.6 broadcast.50
  116.5 5.4 %copy.14 = f32[128,8,8,128]{3,1,2,0:T(8,128)} copy(f32[128,8,8,128]{3,2,1,0:T(8,128)} %bitcast.240) | data formatting | bytes 8388608
  122.2 113.0 %all-reduce.5.cloned.1.call-done = f32[512,1024]{1,0:T(8,128)} async-done(((f32[512,1024]{1,0:T(8,128)}), f32[512,1024]{1,0:T(8,128)}) %all-reduce.5.cloned.1.call-update) | async-done | bytes 2097168 | tf_op jit(solution)/shard_map/psum | solution.py:96
  235.2 2.4 conditional.5
  235.2 1.2 broadcast.52
  236.4 1.1 reshape.54
  237.5 6.3 %maximum_select_fusion = f32[1376256]{0:T(1024)} fusion(f32[327680]{0:T(1024)S(1)} %bitcast.246, f32[1048576]{0:T(1024)} %bitcast.241, f32[327680]{0:T(1024)} %get-tuple-element.66, f32[1048576]{0:T(1024)} %get-tuple-element.62, pred[]{:T(512)S(6)} %eq.4), kind=kLoop, calls=%fused_computation.125 | loop fusion | flops 4128768 | bytes 16515073 | tf_op jit(solution)/shard_map/jit(_where)/select_n | solution.py:118
  243.9 37.5 %collective-permute-start.2 = (f32[1376256]{0:T(1024)}, f32[1376256]{0:T(1024)}, u32[]{:S(2)}, u32[]{:S(2)}) collective-permute-start(f32[1376256]{0:T(1024)} %maximum_select_fusion), channel_id=1, source_target_pairs={{0,16},{16,0},{1,17},{17,1},{2,18},{18,2},{3,19},{19,3},{4,20},{20... | collective-permute-start | bytes 16515080 | tf_op jit(solution)/shard_map/ppermute | solution.py:30
  281.6 4.4 collective-permute-start.1
  286.0 1.6 pad_maximum_fusion
  287.6 2.6 collective-permute-done
  290.2 3.1 concatenate.13
  293.3 3.4 conditional.3
  293.6 0.7 multiply_add_fusion
  294.3 2.5 multiply_add_fusion.1
  296.8 3.2 broadcast_select_fusion
  300.7 107.6 %all-reduce.3.cloned.1.call-done = f32[512,1024]{1,0:T(8,128)} async-done(((f32[512,1024]{1,0:T(8,128)}), f32[512,1024]{1,0:T(8,128)}) %all-reduce.3.cloned.1.call-update) | async-done | bytes 2097168 | tf_op jit(solution)/shard_map/psum | solution.py:26
  408.2 4.4 gather_fusion
  412.6 3.2 select_bitcast_fusion.1
  415.8 28.6 %collective-permute-done.2 = f32[1376256]{0:T(1024)} collective-permute-done((f32[1376256]{0:T(1024)}, f32[1376256]{0:T(1024)}, u32[]{:S(2)}, u32[]{:S(2)}) %collective-permute-start.2) | collective-permute-done | bytes 5505056 | tf_op jit(solution)/shard_map/ppermute | solution.py:30
  444.4 1.4 slice.144
  446.1 4.4 slice.143
  450.5 5.1 %slice.132 = f32[1024,1024]{1,0:T(8,128)} reshape(f32[1048576]{0:T(1024)} %slice.143) | data formatting | bytes 8388608 | tf_op jit(solution)/shard_map/slice | solution.py:121
  455.6 3.0 fusion.100
  458.6 7.1 %select_bitcast_fusion = f32[1,1024,1024]{2,1,0:T(8,128)} fusion(f32[1024,1024]{1,0:T(8,128)} %get-tuple-element.67, f32[1024,1024]{1,0:T(8,128)} %slice.132, pred[]{:T(512)S(6)} %eq.4, f32[1,1024,1024]{2,1,0:T(8,128)S(1)} %copy-done), kind=kLoop, calls=%fused_computation.126 | loop fusion | flops 7340032 | bytes 16777216 | tf_op jit(solution)/shard_map/broadcast_in_dim | solution.py:134
  (29 shorter events, 1.6 us)
Async XLA Ops:
  8.0 93.9 %copy-start.4 = (f32[1,512,1024]{2,1,0:T(8,128)S(1)}, f32[1,512,1024]{2,1,0:T(8,128)}, u32[]{:S(2)}) copy-start(f32[1,512,1024]{2,1,0:T(8,128)} %param.13) | copy-start | bytes 6291460
  8.0 93.9 %all-gather.2.cloned.1.call-start = ((), (), s32[]{:S(2)}) async-start(), calls=%async_computation.1 | async-start | bytes 11141120 | tf_op jit(solution)/shard_map/all_gather | solution.py:72
  10.5 224.7 %all-reduce.5.cloned.1.call-start = ((), (), s32[]{:S(2)}) async-start(), calls=%async_computation.2 | async-start | bytes 4194304 | tf_op jit(solution)/shard_map/psum | solution.py:96
  116.4 291.8 %all-reduce.3.cloned.1.call-start = ((), (), s32[]{:S(2)}) async-start(), calls=%async_computation | async-start | bytes 4194304 | tf_op jit(solution)/shard_map/psum | solution.py:26
  116.5 5.4 %copy-start.2 = (f32[1,5,64,1024]{3,2,1,0:T(8,128)S(1)}, f32[1,5,64,1024]{3,2,1,0:T(8,128)}, u32[]{:S(2)}) copy-start(f32[1,5,64,1024]{3,2,1,0:T(8,128)} %param.19) | copy-start | bytes 3932164
  237.5 43.8 %copy-start.11 = (f32[1024]{0:T(1024)S(1)}, f32[1024]{0:T(1024)}, u32[]{:S(2)}) copy-start(f32[1024]{0:T(1024)} %param.14) | copy-start | bytes 12292
  243.9 200.6 %collective-permute-start.2 = (f32[1376256]{0:T(1024)}, f32[1376256]{0:T(1024)}, u32[]{:S(2)}, u32[]{:S(2)}) collective-permute-start(f32[1376256]{0:T(1024)} %maximum_select_fusion), channel_id=1, source_target_pairs={{0,16},{16,0},{1,17},{17,1},{2,18},{18,2},{3,19},{19,3},{4,20},{20... | collective-permute-start | bytes 16515080 | tf_op jit(solution)/shard_map/ppermute | solution.py:30
  281.5 8.7 %collective-permute-start = (f32[513,1]{1,0:T(8,128)S(1)}, f32[513,1]{1,0:T(8,128)S(1)}, u32[]{:S(2)}, u32[]{:S(2)}) collective-permute-start(f32[513,1]{1,0:T(8,128)S(1)} %get-tuple-element.91), channel_id=1, source_target_pairs={{0,1},{1,2},{2,3},{3,4},{4,5},{5,6},{6,7},{7,8},{8,9},{9,10},{10,1... | collective-permute-start | bytes 6164 | tf_op jit(solution)/shard_map/ppermute | solution.py:18
  281.6 8.6 %collective-permute-start.1 = (f32[513,1]{1,0:T(8,128)S(1)}, f32[513,1]{1,0:T(8,128)S(1)}, u32[]{:S(2)}, u32[]{:S(2)}) collective-permute-start(f32[513,1]{1,0:T(8,128)S(1)} %get-tuple-element.90), channel_id=1, source_target_pairs={{1,0},{2,1},{3,2},{4,3},{5,4},{6,5},{7,6},{8,7},{9,8},{10,9},{11,1... | collective-permute-start | bytes 6164 | tf_op jit(solution)/shard_map/ppermute | solution.py:19
  287.6 5.7 %copy-start.13 = (f32[1024]{0:T(1024)S(1)}, f32[1024]{0:T(1024)}, u32[]{:S(2)}) copy-start(f32[1024]{0:T(1024)} %param.15) | copy-start | bytes 12292
  300.0 0.7 copy-start.12
  450.5 5.1 %copy-start.3 = (f32[1,5,64,1024]{3,2,1,0:T(8,128)S(1)}, f32[1,5,64,1024]{3,2,1,0:T(8,128)}, u32[]{:S(2)}) copy-start(f32[1,5,64,1024]{3,2,1,0:T(8,128)} %param.19) | copy-start | bytes 3932164
  455.6 3.0 copy-start
Sparse Core Ops, SparseCore 0:
  11.6 90.2 all-gather.1
  116.6 118.5 all-reduce.4
Sparse Core Ops, SparseCore 1:
  300.1 108.1 all-reduce.2
where the time goes:
time: 473 us
  waiting for transfers between devices  343 us (73%)
  starting transfers between devices  42.1 us (9%)
  local copies, waits for them, and re-layouts  41.8 us (9%)
  other arithmetic  30.1 us (6%)
  between operations  15.6 us (3%)
    psum x1, waiting for transfers between devices, body(): upstream = lax.psum(partial_grad, 'tile')  113 us
    psum x1, waiting for transfers between devices, spread(): return lax.psum(block, axis)  108 us
    all_gather x1, waiting for transfers between devices, body(): full_hidden = lax.all_gather(hidden_narrow, 'tile', axis=1, tiled=True)  91.3 us
    ppermute x1, starting transfers between devices, partner(): lax.ppermute(value, axis, [(i, i ^ 1 << distance) for i in range(lax.axis...  37.5 us
    ppermute x1, waiting for transfers between devices, partner(): lax.ppermute(value, axis, [(i, i ^ 1 << distance) for i in range(lax.axis...  28.6 us
    another operation x5, local copies, waits for them, and re-layouts  13.6 us
    broadcast_in_dim x3, other arithmetic, body(): return (fields_next[None], out_next[None], hidden_next[None])  13.2 us
    slice x2, local copies, waits for them, and re-layouts, body(): other_out = received[:out_length].reshape(own_out.shape)  9.5 us
  transfers between devices with their start and end apart: 6, of which 5 were waited for; matrix products, arithmetic and copies ran while one was open for 5% of the time, Pallas kernels for 0%

commit v1 on v0

--- a/solution.py
+++ b/solution.py
@@ -93,7 +93,13 @@
     summed_all, inputs_all, grad_out, partial_grad = guarded(
         trainer_side, forward, features, full_hidden, out_narrow, own_fields
     )
-    upstream = lax.psum(partial_grad, "tile")
+    num = lax.axis_size("tile")
+    upstream = partial_grad
+    for to_i in [
+        [(src_i, src_i ^ ii) for src_i in range(num)] for ii in (1, 2, 4, 8, 16) if ii < num
+    ]:
+        arr_now = lax.ppermute(upstream, "tile", to_i)
+        upstream = upstream + arr_now
 
     def backward(summed_all, inputs_all, upstream, full_hidden, first_unit):
         gradients = []

time: 473 us -> 563 us (1.19)
  waiting for transfers between devices: 343 us -> 413 us
  starting transfers between devices: 42.1 us -> 66.8 us
  local copies, waits for them, and re-layouts: 41.8 us -> 34.6 us
    ppermute x0 -> x4, waiting for transfers between devices: none -> 182 us  [body(): arr_now = lax.ppermute(upstream, 'tile', to_i)]
    psum x1 -> x0, waiting for transfers between devices: 113 us -> none  [body(): upstream = lax.psum(partial_grad, 'tile')]
    ppermute x1, starting transfers between devices: 37.5 us -> 58.9 us  [partner(): lax.ppermute(value, axis, [(i, i ^ 1 << distance) for i in range(lax.axis...]
  transfers between devices with their start and end apart: 6 -> 9, of which waited for: 5 -> 8; matrix products, arithmetic and copies ran while one was open for 5% -> 4% of each run, Pallas kernels for 0% -> 0%
where the time goes in v1:
time: 563 us; the launch traced here: 562 us
  waiting for transfers between devices  413 us (73%)
  starting transfers between devices  66.8 us (12%)
  local copies, waits for them, and re-layouts  34.6 us (6%)
  other arithmetic  31.5 us (6%)
  between operations  15.6 us (3%)
    ppermute x4, waiting for transfers between devices, body(): arr_now = lax.ppermute(upstream, 'tile', to_i)  182 us
    psum x1, waiting for transfers between devices, spread(): return lax.psum(block, axis)  108 us
    all_gather x1, waiting for transfers between devices, body(): full_hidden = lax.all_gather(hidden_narrow, 'tile', axis=1, tiled=True)  91.3 us
    ppermute x1, starting transfers between devices, partner(): lax.ppermute(value, axis, [(i, i ^ 1 << distance) for i in range(lax.axis...  58.9 us
    ppermute x1, waiting for transfers between devices, partner(): lax.ppermute(value, axis, [(i, i ^ 1 << distance) for i in range(lax.axis...  29.6 us
    broadcast_in_dim x3, other arithmetic, body(): return (fields_next[None], out_next[None], hidden_next[None])  13.2 us
  transfers between devices with their start and end apart: 9, of which 8 were waited for; matrix products, arithmetic and copies ran while one was open for 4% of the time, Pallas kernels for 0%

profile of v1, /device:TPU:0, one launch (start us, length us, event | category | flops | bytes accessed | tf_op | source)
XLA Modules:
  0.0 562.2 jit_solution(3820966471867848347)
XLA Ops:
  8.1 2.4 bitcast_convert_fusion
  10.5 91.3 %all-gather.2.cloned.1.call-done = bf16[5,1024,1024]{2,1,0:T(8,128)(2,1)} async-done(((bf16[5,64,1024]{2,1,0:T(8,128)(2,1)}), bf16[5,1024,1024]{2,1,0:T(8,128)(2,1)}) %all-gather.2.cloned.1.call-update) | async-done | bytes 10485776 | tf_op jit(solution)/shard_map/all_gather | solution.py:72
  101.9 7.6 %conditional.4 = (f32[5,512,1024]{2,1,0:T(8,128)S(1)}, bf16[5,512,1024]{2,1,0:T(8,128)(2,1)}, f32[1024,1024]{1,0:T(8,128)}, f32[512,1024]{1,0:T(8,128)S(1)}, f32[1048576]{0:T(1024)S(1)}) conditional(s32[]{:T(128)} %convert_element_type.53, () %tuple.39, (bf16[5,1024,1024]{2,1,0:T(8,128)(2,1)}, bf16[512,1024]{1,0:T(8,128)(2,1)}, ...), branch_computations={%region_3.4_spmd, %region_4.5_spmd} | conditional | flops 8619819008 | bytes 199229664 | solution.py:38
  101.9 1.3 broadcast.47
  103.2 3.0 broadcast.48
  106.2 2.5 broadcast.49
  109.8 3.9 collective-permute-done.2
  114.7 47.2 %collective-permute-done.3 = f32[512,1024]{1,0:T(8,128)S(1)} collective-permute-done((f32[512,1024]{1,0:T(8,128)S(1)}, f32[512,1024]{1,0:T(8,128)S(1)}, u32[]{:S(2)}, u32[]{:S(2)}) %collective-permute-start.3) | collective-permute-done | bytes 2097184 | tf_op jit(solution)/shard_map/ppermute | solution.py:101
  163.1 46.2 %collective-permute-done.4 = f32[512,1024]{1,0:T(8,128)S(1)} collective-permute-done((f32[512,1024]{1,0:T(8,128)S(1)}, f32[512,1024]{1,0:T(8,128)S(1)}, u32[]{:S(2)}, u32[]{:S(2)}) %collective-permute-start.4) | collective-permute-done | bytes 2097184 | tf_op jit(solution)/shard_map/ppermute | solution.py:101
  209.9 1.6 collective-permute-start.5
  211.4 5.3 copy.14
  217.0 85.0 %collective-permute-done.5 = f32[512,1024]{1,0:T(8,128)} collective-permute-done((f32[512,1024]{1,0:T(8,128)S(1)}, f32[512,1024]{1,0:T(8,128)}, u32[]{:S(2)}, u32[]{:S(2)}) %collective-permute-start.5) | collective-permute-done | bytes 2097184 | tf_op jit(solution)/shard_map/ppermute | solution.py:101
  302.0 2.3 conditional.5
  302.0 1.2 broadcast.52
  304.3 6.5 %maximum_select_fusion = f32[1376256]{0:T(1024)} fusion(f32[327680]{0:T(1024)S(1)} %bitcast.250, f32[1048576]{0:T(1024)} %bitcast.242, f32[327680]{0:T(1024)} %get-tuple-element.72, f32[1048576]{0:T(1024)} %copy-done.3, pred[]{:T(512)S(6)} %eq.4), kind=kLoop, calls=%fused_computation.125 | loop fusion | flops 4128768 | bytes 16515073 | tf_op jit(solution)/shard_map/jit(_where)/select_n | solution.py:124
  310.8 58.9 %collective-permute-start.6 = (f32[1376256]{0:T(1024)}, f32[1376256]{0:T(1024)}, u32[]{:S(2)}, u32[]{:S(2)}) collective-permute-start(f32[1376256]{0:T(1024)} %maximum_select_fusion), channel_id=1, source_target_pairs={{0,16},{16,0},{1,17},{17,1},{2,18},{18,2},{3,19},{19,3},{4,20},{20... | collective-permute-start | bytes 16515080 | tf_op jit(solution)/shard_map/ppermute | solution.py:30
  369.9 4.4 collective-permute-start.1
  374.3 1.6 pad_maximum_fusion
  375.9 2.6 collective-permute-done
  378.5 3.1 concatenate.13
  381.6 3.2 conditional.3
  382.4 2.5 multiply_add_fusion.1
  384.9 3.2 broadcast_select_fusion
  388.7 107.6 %all-reduce.2.cloned.1.call-done = f32[512,1024]{1,0:T(8,128)} async-done(((f32[512,1024]{1,0:T(8,128)}), f32[512,1024]{1,0:T(8,128)}) %all-reduce.2.cloned.1.call-update) | async-done | bytes 2097168 | tf_op jit(solution)/shard_map/psum | solution.py:26
  496.3 4.4 gather_fusion
  500.7 3.2 select_bitcast_fusion.1
  503.9 29.6 %collective-permute-done.6 = f32[1376256]{0:T(1024)} collective-permute-done((f32[1376256]{0:T(1024)}, f32[1376256]{0:T(1024)}, u32[]{:S(2)}, u32[]{:S(2)}) %collective-permute-start.6) | collective-permute-done | bytes 5505056 | tf_op jit(solution)/shard_map/ppermute | solution.py:30
  533.5 1.4 slice.144
  535.1 4.4 slice.143
  539.6 5.1 slice.132
  544.7 3.0 fusion.100
  547.7 7.1 %select_bitcast_fusion = f32[1,1024,1024]{2,1,0:T(8,128)} fusion(f32[1024,1024]{1,0:T(8,128)} %get-tuple-element.73, f32[1024,1024]{1,0:T(8,128)} %slice.132, pred[]{:T(512)S(6)} %eq.4, f32[1,1024,1024]{2,1,0:T(8,128)S(1)} %copy-done), kind=kLoop, calls=%fused_computation.126 | loop fusion | flops 7340032 | bytes 16777216 | tf_op jit(solution)/shard_map/broadcast_in_dim | solution.py:140
  (43 shorter events, 6.9 us)
Async XLA Ops:
  8.0 93.9 %copy-start.8 = (f32[1,512,1024]{2,1,0:T(8,128)S(1)}, f32[1,512,1024]{2,1,0:T(8,128)}, u32[]{:S(2)}) copy-start(f32[1,512,1024]{2,1,0:T(8,128)} %param.13) | copy-start | bytes 6291460
  8.0 93.9 %all-gather.2.cloned.1.call-start = ((), (), s32[]{:S(2)}) async-start(), calls=%async_computation.1 | async-start | bytes 11141120 | tf_op jit(solution)/shard_map/all_gather | solution.py:72
  10.5 485.8 %all-reduce.2.cloned.1.call-start = ((), (), s32[]{:S(2)}) async-start(), calls=%async_computation | async-start | bytes 4194304 | tf_op jit(solution)/shard_map/psum | solution.py:26
  109.4 4.6 copy-start.3
  109.4 52.9 %copy-start.5 = (f32[5,512,1024]{2,1,0:T(8,128)}, f32[5,512,1024]{2,1,0:T(8,128)S(1)}, u32[]{:S(2)}) copy-start(f32[5,512,1024]{2,1,0:T(8,128)S(1)} %get-tuple-element.71) | copy-start | bytes 31457284
  109.5 4.2 collective-permute-start.2
  114.1 47.9 %collective-permute-start.3 = (f32[512,1024]{1,0:T(8,128)S(1)}, f32[512,1024]{1,0:T(8,128)S(1)}, u32[]{:S(2)}, u32[]{:S(2)}) collective-permute-start(f32[512,1024]{1,0:T(8,128)S(1)} %add.111), channel_id=1, source_target_pairs={{0,2},{1,3},{2,0},{3,1},{4,6},{5,7},{6,4},{7,5},{8,10},{9,11},{10,... | collective-permute-start | bytes 6291464 | tf_op jit(solution)/shard_map/ppermute | solution.py:101
  162.3 47.0 %collective-permute-start.4 = (f32[512,1024]{1,0:T(8,128)S(1)}, f32[512,1024]{1,0:T(8,128)S(1)}, u32[]{:S(2)}, u32[]{:S(2)}) collective-permute-start(f32[512,1024]{1,0:T(8,128)S(1)} %add.112), channel_id=1, source_target_pairs={{0,4},{1,5},{2,6},{3,7},{4,0},{5,1},{6,2},{7,3},{8,12},{9,13},{10,... | collective-permute-start | bytes 6291464 | tf_op jit(solution)/shard_map/ppermute | solution.py:101
  209.9 92.1 %collective-permute-start.5 = (f32[512,1024]{1,0:T(8,128)S(1)}, f32[512,1024]{1,0:T(8,128)}, u32[]{:S(2)}, u32[]{:S(2)}) collective-permute-start(f32[512,1024]{1,0:T(8,128)S(1)} %add.113), channel_id=1, source_target_pairs={{0,8},{1,9},{2,10},{3,11},{4,12},{5,13},{6,14},{7,15},{8,0},{9,1},... | collective-permute-start | bytes 6291464 | tf_op jit(solution)/shard_map/ppermute | solution.py:101
  211.4 5.3 copy-start.6
  304.3 65.4 %copy-start.9 = (f32[1,512,1024]{2,1,0:T(8,128)S(1)}, f32[1,512,1024]{2,1,0:T(8,128)}, u32[]{:S(2)}) copy-start(f32[1,512,1024]{2,1,0:T(8,128)} %param.13) | copy-start | bytes 6291460
  304.3 65.4 %copy-start.16 = (f32[1024]{0:T(1024)S(1)}, f32[1024]{0:T(1024)}, u32[]{:S(2)}) copy-start(f32[1024]{0:T(1024)} %param.14) | copy-start | bytes 12292
  310.8 222.8 %collective-permute-start.6 = (f32[1376256]{0:T(1024)}, f32[1376256]{0:T(1024)}, u32[]{:S(2)}, u32[]{:S(2)}) collective-permute-start(f32[1376256]{0:T(1024)} %maximum_select_fusion), channel_id=1, source_target_pairs={{0,16},{16,0},{1,17},{17,1},{2,18},{18,2},{3,19},{19,3},{4,20},{20... | collective-permute-start | bytes 16515080 | tf_op jit(solution)/shard_map/ppermute | solution.py:30
  369.8 8.7 %collective-permute-start = (f32[513,1]{1,0:T(8,128)S(1)}, f32[513,1]{1,0:T(8,128)S(1)}, u32[]{:S(2)}, u32[]{:S(2)}) collective-permute-start(f32[513,1]{1,0:T(8,128)S(1)} %get-tuple-element.97), channel_id=1, source_target_pairs={{0,1},{1,2},{2,3},{3,4},{4,5},{5,6},{6,7},{7,8},{8,9},{9,10},{10,1... | collective-permute-start | bytes 6164 | tf_op jit(solution)/shard_map/ppermute | solution.py:18
  369.9 8.6 %collective-permute-start.1 = (f32[513,1]{1,0:T(8,128)S(1)}, f32[513,1]{1,0:T(8,128)S(1)}, u32[]{:S(2)}, u32[]{:S(2)}) collective-permute-start(f32[513,1]{1,0:T(8,128)S(1)} %get-tuple-element.96), channel_id=1, source_target_pairs={{1,0},{2,1},{3,2},{4,3},{5,4},{6,5},{7,6},{8,7},{9,8},{10,9},{11,1... | collective-permute-start | bytes 6164 | tf_op jit(solution)/shard_map/ppermute | solution.py:19
  375.9 5.7 %copy-start.18 = (f32[1024]{0:T(1024)S(1)}, f32[1024]{0:T(1024)}, u32[]{:S(2)}) copy-start(f32[1024]{0:T(1024)} %param.15) | copy-start | bytes 12292
  388.0 0.7 copy-start.17
  539.6 5.1 copy-start.7
  544.7 3.0 copy-start
Sparse Core Ops, SparseCore 0:
  11.6 90.2 all-gather.1
Sparse Core Ops, SparseCore 1:
  388.1 108.1 all-reduce.1
